TPU v7x, 256 devices: a whole 4x4x8 slice. The times are simulated.
256 devices in a mesh: probe: 64 (over z, x_lo, y), slab: 4 (over x_hi, core).
Axes of the slice: x: 4 (x_hi: 2, x_lo: 2; x = x_hi * 2 + x_lo), y: 4, z: 8, core: 2. Of those that a mesh axis runs over, the one named last changes fastest.
Arguments:
- smatrix: bfloat16 [2, 512, 128, 128], P(None, 'probe', 'slab'), may hold values from -6 to 6
- amplitude: float32 [2, 512], replicated, may hold values from -0.25 to 0.25
- beam_index: int32 [512, 2], replicated, may hold values from -32 to 31
- positions: int32 [8192, 2], P('probe'), may hold values from -8 to 8
Outputs:
- patterns: float32 [8192, 128, 128], P('probe', 'slab')
Inputs may be any that keep to these rules, and one draw needn't show every extreme that they name: `positions`: column 0 is the row offset that places a probe's crop in the band, column 1 the column offset. `beam_index`: column 0 along rows, column 1 along columns.
All inputs are finite; a program needn't handle non-finite values.
Results may differ from a plain program's by a relative error of at most 0.0029.
Values may be sent and summed in bfloat16 or wider, within the bound.
A program may use at most 128 MiB of HBM per device.

v0:
```python
import math
import jax
import jax.numpy as jnp
from jax import lax
from jax.sharding import PartitionSpec as P

HALO = 8


def padded_2(x, sides, width):
    for axis, dim in sides:
        count, length = (lax.axis_size(axis), x.shape[dim])
        up = [(i, (i + 1) % count) for i in range(count - 1)]
        down = [(j, i) for i, j in up]
        last = lax.slice_in_dim(x, length - width, length, axis=dim)
        leading = lax.slice_in_dim(x, 0, width, axis=dim)
        before = lax.ppermute(last, axis, up)
        after = lax.ppermute(leading, axis, down)
        x = jnp.concatenate([before, x, after], axis=dim)
    return x


def beam_weights(amplitude, beam_index, place, rows_all, cols):
    row_phase = (
        jnp.mod(place[:, 0:1] * beam_index[None, :, 0], rows_all).astype(jnp.float32) / rows_all
    )
    col_phase = jnp.mod(place[:, 1:2] * beam_index[None, :, 1], cols).astype(jnp.float32) / cols
    angle = 2.0 * math.pi * (row_phase + col_phase)
    cosine = jnp.cos(angle)
    sine = jnp.sin(angle)
    real = amplitude[0][None, :] * cosine + amplitude[1][None, :] * sine
    imag = amplitude[1][None, :] * cosine - amplitude[0][None, :] * sine
    return (real.astype(jnp.bfloat16), imag.astype(jnp.bfloat16))


def dft_table(first, second, length):
    angle = (
        2.0
        * math.pi
        * (jnp.mod(first[:, None] * second[None, :], length).astype(jnp.float32) / length)
    )
    return (jnp.cos(angle), jnp.sin(angle))


def cut_rows(field, offset, count):
    return lax.dynamic_slice_in_dim(field, offset, count, 0)


def on_device(smatrix, amplitude, beam_index, positions):
    slab_rows = smatrix.shape[2]
    cols = smatrix.shape[3]
    rows_all = slab_rows * lax.axis_size("slab")
    probes_here = positions.shape[0]
    tall = slab_rows + 2 * HALO
    band = tall * cols
    highest = lax.Precision.HIGHEST
    weight_re, weight_im = beam_weights(amplitude, beam_index, positions, rows_all, cols)
    padded = padded_2(smatrix, (("slab", 2),), HALO)
    piece = lax.all_gather(padded, "probe", axis=1, tiled=True)
    count = piece.shape[1]
    flat = piece.reshape(2, count, band)
    real = jnp.dot(weight_re, flat[0], preferred_element_type=jnp.float32) - jnp.dot(
        weight_im, flat[1], preferred_element_type=jnp.float32
    )
    imag = jnp.dot(weight_re, flat[1], preferred_element_type=jnp.float32) + jnp.dot(
        weight_im, flat[0], preferred_element_type=jnp.float32
    )
    starts = positions[:, 0] + HALO
    wave_re = jax.vmap(lambda field, offset: cut_rows(field, offset, slab_rows))(
        real.reshape(probes_here, tall, cols), starts
    )
    wave_im = jax.vmap(lambda field, offset: cut_rows(field, offset, slab_rows))(
        imag.reshape(probes_here, tall, cols), starts
    )
    col_index = jnp.arange(cols, dtype=jnp.int32)
    col_cos, col_sin = dft_table(col_index, col_index, cols)
    half_re = jnp.dot(wave_re, col_cos, precision=highest) + jnp.dot(
        wave_im, col_sin, precision=highest
    )
    half_im = jnp.dot(wave_im, col_cos, precision=highest) - jnp.dot(
        wave_re, col_sin, precision=highest
    )
    scale = 1.0 / math.sqrt(rows_all * cols)
    local_rows = lax.axis_index("slab") * slab_rows + jnp.arange(slab_rows, dtype=jnp.int32)
    freq = jnp.arange(lax.axis_size("slab") * slab_rows, dtype=jnp.int32)
    row_cos, row_sin = dft_table(freq, local_rows, rows_all)
    out_re = jnp.einsum("kr,prc->kpc", row_cos, half_re, precision=highest) + jnp.einsum(
        "kr,prc->kpc", row_sin, half_im, precision=highest
    )
    out_im = jnp.einsum("kr,prc->kpc", row_cos, half_im, precision=highest) - jnp.einsum(
        "kr,prc->kpc", row_sin, half_re, precision=highest
    )
    summed = lax.psum_scatter(
        jnp.stack([out_re, out_im], 1) * scale, "slab", scatter_dimension=0, tiled=True
    )
    power = summed[:, 0] ** 2 + summed[:, 1] ** 2
    return jnp.transpose(power, (1, 0, 2))


def solution(mesh):
    return jax.shard_map(
        on_device,
        mesh=mesh,
        in_specs=(P(None, "probe", "slab", None), P(), P(), P("probe", None)),
        out_specs=P("probe", "slab", None),
        check_vma=False,
    )
```

profile of v0, /device:TPU:1, one launch (start us, length us, event | category | flops | bytes accessed | tf_op | source)
XLA Modules:
  0.0 566.4 jit_solution(1741276528891264881)
XLA Ops:
  6.5 0.8 fusion.116
  7.3 6.0 %collective-permute-start = (bf16[2,8,8,128]{3,2,1,0:T(8,128)(2,1)S(1)}, bf16[2,8,8,128]{3,2,1,0:T(8,128)(2,1)S(1)}, u32[]{:S(2)}, u32[]{:S(2)}) collective-permute-start(bf16[2,8,8,128]{3,2,1,0:T(8,128)(2,1)S(1)} %get-tuple-element.7), channel_id=1, source_target_pairs={{0,1},{1,2},{2,3},{4,5},{5,6},{6,7},{8,9},{9,10},{10,11},{12,13},{... | collective-permute-start | bytes 98312 | tf_op jit(solution)/shard_map/ppermute | solution.py:17
  13.3 1.9 collective-permute-start.1
  15.3 4.8 collective-permute-done.1
  20.1 1.6 pad_maximum_fusion
  21.7 0.0 all-gather.2.cloned.1.call-update
  21.7 0.0 reduce-scatter.2.cloned.1.call-start
  21.8 0.8 or_bitcast_fusion
  22.5 0.8 fusion.117
  23.3 0.8 fusion.118
  24.1 276.4 %all-gather.2.cloned.1.call-done = bf16[2,512,48,128]{3,2,1,0:T(8,128)(2,1)} async-done(((bf16[2,8,48,128]{3,2,1,0:T(8,128)(2,1)}), bf16[2,512,48,128]{3,2,1,0:T(8,128)(2,1)}) %all-gather.2.cloned.1.call-update) | async-done | bytes 12582928 | tf_op jit(solution)/shard_map/all_gather | solution.py:59
  300.5 6.2 %fusion.115 = (bf16[1,512,48,128]{3,2,1,0:T(8,128)(2,1)S(1)}, bf16[1,512,48,128]{3,2,1,0:T(8,128)(2,1)S(1)}) fusion(bf16[2,512,48,128]{3,2,1,0:T(8,128)(2,1)} %all-gather.2.cloned.1.call-done), kind=kLoop, calls=%fused_computation.140 | loop fusion | bytes 25165824 | tf_op jit(solution)/shard_map/slice | solution.py:62
  306.7 2.4 fusion
  309.1 2.4 fusion.4
  311.4 2.6 fusion.21
  314.0 2.6 fusion.18
  316.6 2.0 copy.46
  318.7 0.4 copy.45
  319.1 6.3 %gather_fusion = f32[128,32,128]{2,0,1:T(8,128)} fusion(f32[128,48,128]{2,0,1:T(8,128)} %bitcast.71, s32[128]{0:T(128)S(1)} %get-tuple-element.13), kind=kCustom, calls=%fused_computation | custom fusion | bytes 4195840 | tf_op jit(solution)/shard_map/vmap()/gather | solution.py:46
  325.4 6.2 %gather_fusion.1 = f32[128,32,128]{2,0,1:T(8,128)} fusion(f32[128,48,128]{2,0,1:T(8,128)S(1)} %bitcast.70, s32[128]{0:T(128)S(1)} %get-tuple-element.13), kind=kCustom, calls=%fused_computation.1 | custom fusion | bytes 4195840 | tf_op jit(solution)/shard_map/vmap()/gather | solution.py:46
  331.6 3.9 fusion.37
  335.5 2.1 fusion.39
  337.7 2.1 convolution_subtract_fusion.1
  339.8 2.3 convolution_add_fusion.1
  342.1 7.4 %fusion.16 = f32[128,128,128]{2,0,1:T(8,128)S(1)} fusion(f32[128,32,128]{2,0,1:T(8,128)S(1)} %convolution_add_fusion.1, s32[32]{0:T(128)S(1)} %iota_add_fusion), kind=kOutput, calls=%fused_computation.27 | convolution fusion | flops 805363712 | bytes 10485888 | tf_op jit(solution)/shard_map/kr,prc->kpc/dot_general | solution.py:87
  349.5 7.7 %fusion.12 = f32[128,128,128]{2,0,1:T(8,128)S(1)} fusion(f32[128,32,128]{2,0,1:T(8,128)S(1)} %convolution_subtract_fusion.1, s32[32]{0:T(128)S(1)} %iota_add_fusion), kind=kOutput, calls=%fused_computation.23 | convolution fusion | flops 805363712 | bytes 10485888 | tf_op jit(solution)/shard_map/kr,prc->kpc/dot_general | solution.py:90
  357.2 7.4 %add_bitcast_fusion = f32[128,1,128,128]{3,0,2,1:T(8,128)S(1)} fusion(f32[128,128,128]{2,0,1:T(8,128)S(1)} %fusion.16, f32[128,32,128]{2,0,1:T(8,128)S(1)} %convolution_subtract_fusion.1, s32[32]{0:T(128)S(1)} %iota_add_fusion), kind=kOutput, calls=%fused_computation.4 | convolution fusion | flops 807460864 | bytes 18874496 | tf_op jit(solution)/shard_map/kr,prc->kpc/dot_general | solution.py:87
  364.6 7.7 %subtract_bitcast_fusion = f32[128,1,128,128]{3,0,2,1:T(8,128)S(1)} fusion(f32[128,128,128]{2,0,1:T(8,128)S(1)} %fusion.12, f32[128,32,128]{2,0,1:T(8,128)S(1)} %convolution_add_fusion.1, s32[32]{0:T(128)S(1)} %iota_add_fusion), kind=kOutput, calls=%fused_computation.3 | convolution fusion | flops 807460864 | bytes 18874496 | tf_op jit(solution)/shard_map/kr,prc->kpc/dot_general | solution.py:90
  372.3 6.0 %maximum_multiply_fusion = f32[128,2,128,128]{3,0,2,1:T(8,128)} fusion(f32[128,1,128,128]{3,0,2,1:T(8,128)S(1)} %subtract_bitcast_fusion, f32[128,1,128,128]{3,0,2,1:T(8,128)S(1)} %add_bitcast_fusion), kind=kLoop, calls=%fused_computation.2 | loop fusion | flops 8388608 | bytes 33554432 | tf_op jit(solution)/shard_map/mul | solution.py:94
  378.4 0.0 reduce-scatter.2.cloned.1.call-update
  378.4 176.7 %reduce-scatter.2.cloned.1.call-done = f32[32,2,128,128]{3,0,2,1:T(8,128)} async-done(((f32[128,2,128,128]{3,0,2,1:T(8,128)}), f32[32,2,128,128]{3,0,2,1:T(8,128)}) %reduce-scatter.2.cloned.1.call-update) | async-done | bytes 4194320 | tf_op jit(solution)/shard_map/reduce_scatter | solution.py:93
  555.1 4.0 fusion.11
  (7 shorter events, 0.0 us)
Async XLA Ops:
  6.5 294.0 %all-gather.2.cloned.1.call-start = ((), (), s32[]{:S(2)}) async-start(), calls=%async_computation.1 | async-start | bytes 12779520 | tf_op jit(solution)/shard_map/all_gather | solution.py:59
  7.3 8.0 %collective-permute-start = (bf16[2,8,8,128]{3,2,1,0:T(8,128)(2,1)S(1)}, bf16[2,8,8,128]{3,2,1,0:T(8,128)(2,1)S(1)}, u32[]{:S(2)}, u32[]{:S(2)}) collective-permute-start(bf16[2,8,8,128]{3,2,1,0:T(8,128)(2,1)S(1)} %get-tuple-element.7), channel_id=1, source_target_pairs={{0,1},{1,2},{2,3},{4,5},{5,6},{6,7},{8,9},{9,10},{10,11},{12,13},{... | collective-permute-start | bytes 98312 | tf_op jit(solution)/shard_map/ppermute | solution.py:17
  13.3 6.7 %collective-permute-start.1 = (bf16[2,8,8,128]{3,2,1,0:T(8,128)(2,1)S(1)}, bf16[2,8,8,128]{3,2,1,0:T(8,128)(2,1)S(1)}, u32[]{:S(2)}, u32[]{:S(2)}) collective-permute-start(bf16[2,8,8,128]{3,2,1,0:T(8,128)(2,1)S(1)} %get-tuple-element.8), channel_id=1, source_target_pairs={{1,0},{2,1},{3,2},{5,4},{6,5},{7,6},{9,8},{10,9},{11,10},{13,12},{... | collective-permute-start | bytes 98312 | tf_op jit(solution)/shard_map/ppermute | solution.py:18
  21.7 533.4 %reduce-scatter.2.cloned.1.call-start = ((), (), s32[]{:S(2)}) async-start(), calls=%async_computation.2 | async-start | bytes 20971520 | tf_op jit(solution)/shard_map/reduce_scatter | solution.py:93
  331.6 3.9 copy-start.1
  337.7 2.1 copy-start
Sparse Core Ops, SparseCore 0:
  21.8 278.6 all-gather.1
  378.5 176.5 reduce-scatter.1
where the time goes:
time: 576 us; the launch traced here: 566 us
  waiting for transfers between devices  458 us (80%)
  matrix products  50.5 us (9%)
  local copies, waits for them, and re-layouts  23.5 us (4%)
  between operations  14 us (2%)
  other arithmetic  12.5 us (2%)
  starting transfers between devices  7.98 us (1%)
    all_gather x1, waiting for transfers between devices, on_device(): piece = lax.all_gather(padded, 'probe', axis=1, tiled=True)  276 us
    reduce_scatter x1, waiting for transfers between devices, on_device(): lax.psum_scatter(jnp.stack([out_re, out_im], 1) * scale, 'slab', scatter_...  177 us
    gather x2, local copies, waits for them, and re-layouts, cut_rows(): return lax.dynamic_slice_in_dim(field, offset, count, 0)  12.6 us
  transfers between devices with their start and end apart: 4, of which 3 were waited for; matrix products, arithmetic and copies ran while one was open for 0% of the time, Pallas kernels for 0%

commit v1 on v0

--- a/solution.py
+++ b/solution.py
@@ -56,7 +56,9 @@
     highest = lax.Precision.HIGHEST
     weight_re, weight_im = beam_weights(amplitude, beam_index, positions, rows_all, cols)
     padded = padded_2(smatrix, (("slab", 2),), HALO)
-    piece = lax.all_gather(padded, "probe", axis=1, tiled=True)
+    piece = jnp.concatenate(
+        lax.all_to_all(jnp.stack([padded] * lax.axis_size("probe")), "probe", 0, 0), axis=1
+    )
     count = piece.shape[1]
     flat = piece.reshape(2, count, band)
     real = jnp.dot(weight_re, flat[0], preferred_element_type=jnp.float32) - jnp.dot(

time: 576 us -> 539 us (0.936)
  waiting for transfers between devices: 458 us -> 409 us
  starting transfers between devices: 7.98 us -> 20.2 us
  local copies, waits for them, and re-layouts: 23.5 us -> 30 us
    all_gather x1 -> x0, waiting for transfers between devices: 276 us -> none  [on_device(): piece = lax.all_gather(padded, 'probe', axis=1, tiled=True)]
    all_to_all x0 -> x1, waiting for transfers between devices: none -> 272 us  [on_device(): lax.all_to_all(jnp.stack([padded] * lax.axis_size('probe')), 'probe', 0, 0)]
    reduce_scatter x1, waiting for transfers between devices: 177 us -> 133 us  [on_device(): lax.psum_scatter(jnp.stack([out_re, out_im], 1) * scale, 'slab', scatter_...]
    all_to_all x0 -> x1, starting transfers between devices: none -> 12.2 us  [on_device(): lax.all_to_all(jnp.stack([padded] * lax.axis_size('probe')), 'probe', 0, 0)]
    another operation x0 -> x1, local copies, waits for them, and re-layouts: none -> 7.61 us  [on_device(): jnp.stack([padded] * lax.axis_size('probe'))]
    unnamed x4 -> x11, local copies, waits for them, and re-layouts: 0.01 us -> 6.73 us
    slice x1 -> x0, local copies, waits for them, and re-layouts: 6.15 us -> none  [on_device(): flat[0]]
where the time goes in v1:
time: 539 us; the launch traced here: 535 us
  waiting for transfers between devices  409 us (76%)
  matrix products  50.7 us (9%)
  local copies, waits for them, and re-layouts  30 us (6%)
  starting transfers between devices  20.2 us (4%)
  between operations  13.9 us (3%)
  other arithmetic  11 us (2%)
    all_to_all x1, waiting for transfers between devices, on_device(): lax.all_to_all(jnp.stack([padded] * lax.axis_size('probe')), 'probe', 0, 0)  272 us
    reduce_scatter x1, waiting for transfers between devices, on_device(): lax.psum_scatter(jnp.stack([out_re, out_im], 1) * scale, 'slab', scatter_...  133 us
    gather x2, local copies, waits for them, and re-layouts, cut_rows(): return lax.dynamic_slice_in_dim(field, offset, count, 0)  12.4 us
    all_to_all x1, starting transfers between devices, on_device(): lax.all_to_all(jnp.stack([padded] * lax.axis_size('probe')), 'probe', 0, 0)  12.2 us
  transfers between devices with their start and end apart: 4, of which 3 were waited for; matrix products, arithmetic and copies ran while one was open for 0% of the time, Pallas kernels for 0%

profile of v1, /device:TPU:1, one launch (start us, length us, event | category | flops | bytes accessed | tf_op | source)
XLA Modules:
  0.0 535.0 jit_solution(4978994689818359028)
XLA Ops:
  6.5 0.8 fusion.115
  7.3 6.0 %collective-permute-start = (bf16[2,8,8,128]{3,2,1,0:T(8,128)(2,1)S(1)}, bf16[2,8,8,128]{3,2,1,0:T(8,128)(2,1)S(1)}, u32[]{:S(2)}, u32[]{:S(2)}) collective-permute-start(bf16[2,8,8,128]{3,2,1,0:T(8,128)(2,1)S(1)} %get-tuple-element.7), channel_id=1, source_target_pairs={{0,1},{1,2},{2,3},{4,5},{5,6},{6,7},{8,9},{9,10},{10,11},{12,13},{... | collective-permute-start | bytes 98312 | tf_op jit(solution)/shard_map/ppermute | solution.py:17
  13.3 1.9 collective-permute-start.1
  15.3 0.0 collective-permute-done
  15.3 4.8 collective-permute-done.1
  20.1 0.9 pad_maximum_fusion
  21.0 7.6 %stack.8 = bf16[64,2,8,48,128]{4,3,2,1,0:T(8,128)(2,1)} broadcast(bf16[2,8,48,128]{3,2,1,0:T(8,128)(2,1)S(1)} %pad_maximum_fusion), dimensions={1,2,3,4} | broadcast | bytes 12779520 | tf_op jit(solution)/shard_map/stack | solution.py:60
  28.6 12.2 %all-to-all-start = ((bf16[64,2,8,48,128]{4,3,2,1,0:T(8,128)(2,1)}), bf16[64,2,8,48,128]{4,3,2,1,0:T(8,128)(2,1)}, u32[]{:S(2)}, u32[]{:S(2)}) async-start(bf16[64,2,8,48,128]{4,3,2,1,0:T(8,128)(2,1)} %stack.8), calls=%async_computation | async-start | bytes 25165824 | tf_op jit(solution)/shard_map/all_to_all | solution.py:60
  40.9 0.0 reduce-scatter.2.cloned.1.call-start
  41.0 271.9 %all-to-all-done = bf16[64,2,8,48,128]{4,3,2,1,0:T(8,128)(2,1)} async-done(((bf16[64,2,8,48,128]{4,3,2,1,0:T(8,128)(2,1)}), bf16[64,2,8,48,128]{4,3,2,1,0:T(8,128)(2,1)}, u32[]{:S(2)}, u32[]{:S(2)}) %all-to-all-start) | async-done | bytes 12582944 | tf_op jit(solution)/shard_map/all_to_all | solution.py:60
  312.9 6.7 %slice_bitcast_fusion.1 = (bf16[64,8,48,128]{3,2,1,0:T(8,128)(2,1)S(1)}, bf16[64,8,48,128]{3,2,1,0:T(8,128)(2,1)S(1)}) fusion(bf16[2,64,8,48,128]{4,3,2,0,1:T(8,128)(2,1)} %bitcast.7), kind=kLoop, calls=%fused_computation.14 | loop fusion | bytes 25165824
  319.6 2.4 fusion.4
  322.0 2.4 fusion
  324.4 2.6 fusion.18
  327.0 2.6 fusion.21
  329.6 2.0 copy.45
  331.6 0.4 copy.46
  332.0 6.2 %gather_fusion.1 = f32[128,32,128]{2,0,1:T(8,128)} fusion(f32[128,48,128]{2,0,1:T(8,128)} %bitcast.76, s32[128]{0:T(128)S(1)} %get-tuple-element.13), kind=kCustom, calls=%fused_computation.1 | custom fusion | bytes 4195840 | tf_op jit(solution)/shard_map/vmap()/gather | solution.py:46
  338.2 6.3 %gather_fusion = f32[128,32,128]{2,0,1:T(8,128)} fusion(f32[128,48,128]{2,0,1:T(8,128)S(1)} %bitcast.75, s32[128]{0:T(128)S(1)} %get-tuple-element.13), kind=kCustom, calls=%fused_computation | custom fusion | bytes 4195840 | tf_op jit(solution)/shard_map/vmap()/gather | solution.py:46
  344.5 3.8 fusion.39
  348.3 0.0 copy-done.1
  348.3 2.1 fusion.37
  350.5 2.1 convolution_add_fusion.1
  352.6 2.5 convolution_subtract_fusion.1
  355.2 7.4 %fusion.12 = f32[128,128,128]{2,0,1:T(8,128)S(1)} fusion(f32[128,32,128]{2,0,1:T(8,128)S(1)} %convolution_subtract_fusion.1, s32[32]{0:T(128)S(1)} %iota_add_fusion), kind=kOutput, calls=%fused_computation.25 | convolution fusion | flops 805363712 | bytes 10485888 | tf_op jit(solution)/shard_map/kr,prc->kpc/dot_general | solution.py:92
  362.6 7.6 %fusion.16 = f32[128,128,128]{2,0,1:T(8,128)S(1)} fusion(f32[128,32,128]{2,0,1:T(8,128)S(1)} %convolution_add_fusion.1, s32[32]{0:T(128)S(1)} %iota_add_fusion), kind=kOutput, calls=%fused_computation.29 | convolution fusion | flops 805363712 | bytes 10485888 | tf_op jit(solution)/shard_map/kr,prc->kpc/dot_general | solution.py:89
  370.2 7.4 %subtract_bitcast_fusion = f32[128,1,128,128]{3,0,2,1:T(8,128)S(1)} fusion(f32[128,128,128]{2,0,1:T(8,128)S(1)} %fusion.12, f32[128,32,128]{2,0,1:T(8,128)S(1)} %convolution_add_fusion.1, s32[32]{0:T(128)S(1)} %iota_add_fusion), kind=kOutput, calls=%fused_computation.3 | convolution fusion | flops 807460864 | bytes 18874496 | tf_op jit(solution)/shard_map/kr,prc->kpc/dot_general | solution.py:92
  377.6 7.7 %add_bitcast_fusion = f32[128,1,128,128]{3,0,2,1:T(8,128)S(1)} fusion(f32[128,128,128]{2,0,1:T(8,128)S(1)} %fusion.16, f32[128,32,128]{2,0,1:T(8,128)S(1)} %convolution_subtract_fusion.1, s32[32]{0:T(128)S(1)} %iota_add_fusion), kind=kOutput, calls=%fused_computation.4 | convolution fusion | flops 807460864 | bytes 18874496 | tf_op jit(solution)/shard_map/kr,prc->kpc/dot_general | solution.py:89
  385.3 6.0 %maximum_multiply_fusion = f32[128,2,128,128]{3,0,2,1:T(8,128)} fusion(f32[128,1,128,128]{3,0,2,1:T(8,128)S(1)} %subtract_bitcast_fusion, f32[128,1,128,128]{3,0,2,1:T(8,128)S(1)} %add_bitcast_fusion), kind=kLoop, calls=%fused_computation.2 | loop fusion | flops 8388608 | bytes 33554432 | tf_op jit(solution)/shard_map/mul | solution.py:96
  391.4 0.0 reduce-scatter.2.cloned.1.call-update
  391.4 132.6 %reduce-scatter.2.cloned.1.call-done = f32[32,2,128,128]{3,0,2,1:T(8,128)} async-done(((f32[128,2,128,128]{3,0,2,1:T(8,128)}), f32[32,2,128,128]{3,0,2,1:T(8,128)}) %reduce-scatter.2.cloned.1.call-update) | async-done | bytes 4194320 | tf_op jit(solution)/shard_map/reduce_scatter | solution.py:95
  523.9 4.0 fusion.11
  (13 shorter events, 0.0 us)
Async XLA Ops:
  7.3 8.0 %collective-permute-start = (bf16[2,8,8,128]{3,2,1,0:T(8,128)(2,1)S(1)}, bf16[2,8,8,128]{3,2,1,0:T(8,128)(2,1)S(1)}, u32[]{:S(2)}, u32[]{:S(2)}) collective-permute-start(bf16[2,8,8,128]{3,2,1,0:T(8,128)(2,1)S(1)} %get-tuple-element.7), channel_id=1, source_target_pairs={{0,1},{1,2},{2,3},{4,5},{5,6},{6,7},{8,9},{9,10},{10,11},{12,13},{... | collective-permute-start | bytes 98312 | tf_op jit(solution)/shard_map/ppermute | solution.py:17
  13.3 6.7 %collective-permute-start.1 = (bf16[2,8,8,128]{3,2,1,0:T(8,128)(2,1)S(1)}, bf16[2,8,8,128]{3,2,1,0:T(8,128)(2,1)S(1)}, u32[]{:S(2)}, u32[]{:S(2)}) collective-permute-start(bf16[2,8,8,128]{3,2,1,0:T(8,128)(2,1)S(1)} %get-tuple-element.8), channel_id=1, source_target_pairs={{1,0},{2,1},{3,2},{5,4},{6,5},{7,6},{9,8},{10,9},{11,10},{13,12},{... | collective-permute-start | bytes 98312 | tf_op jit(solution)/shard_map/ppermute | solution.py:18
  28.6 12.3 %copy-start.4 = (s32[128,2]{0,1:T(2,128)S(1)}, s32[128,2]{0,1:T(2,128)}, u32[]{:S(2)}) copy-start(s32[128,2]{0,1:T(2,128)} %param.7) | copy-start | bytes 3076
  28.6 12.3 %copy-start.2 = (f32[2,512]{1,0:T(2,128)S(1)}, f32[2,512]{1,0:T(2,128)}, u32[]{:S(2)}) copy-start(f32[2,512]{1,0:T(2,128)} %param.5) | copy-start | bytes 12292
  28.6 12.3 %copy-start.3 = (s32[512,2]{0,1:T(2,128)S(1)}, s32[512,2]{0,1:T(2,128)}, u32[]{:S(2)}) copy-start(s32[512,2]{0,1:T(2,128)} %param.6) | copy-start | bytes 12292
  28.6 284.3 %all-to-all-start = ((bf16[64,2,8,48,128]{4,3,2,1,0:T(8,128)(2,1)}), bf16[64,2,8,48,128]{4,3,2,1,0:T(8,128)(2,1)}, u32[]{:S(2)}, u32[]{:S(2)}) async-start(bf16[64,2,8,48,128]{4,3,2,1,0:T(8,128)(2,1)} %stack.8), calls=%async_computation | async-start | bytes 25165824 | tf_op jit(solution)/shard_map/all_to_all | solution.py:60
  40.9 483.1 %reduce-scatter.2.cloned.1.call-start = ((), (), s32[]{:S(2)}) async-start(), calls=%async_computation.2 | async-start | bytes 20971520 | tf_op jit(solution)/shard_map/reduce_scatter | solution.py:95
  344.5 3.9 copy-start.1
  350.5 2.1 copy-start
Sparse Core Ops, SparseCore 0:
  391.5 132.3 reduce-scatter.1
